TPU v7x, 256 devices: a whole 4x4x8 slice. The times are simulated.
256 devices in a mesh: leaf: 64 (over x, z, core), rhs: 4 (over y).
Axes of the slice: x: 4, y: 4, z: 8, core: 2. Of those that a mesh axis runs over, the one named last changes fastest.
Arguments:
- input_columns: float32 [8, 1024, 256], P('rhs', 'leaf'), may hold values from -6 to 6
- near_blocks: float32 [8192, 256, 256], P(('leaf', 'rhs')), may hold values from -0.25 to 0.25
- near_pairs: int32 [8192, 2], P(('leaf', 'rhs')), may hold values from -1 to 1023, as said below
- leaf_basis: float32 [1024, 64, 256], P(('leaf', 'rhs')), may hold values from -0.375 to 0.375
- local_transfer: float32 [1792, 64, 64], P('leaf'), may hold values from -0.5 to 0.5
- local_coupling: float32 [1792, 4, 64, 64], P('leaf'), may hold values from -0.4375 to 0.4375
- local_lists: int32 [1792, 4], P('leaf'), may hold values from -1 to 1023, as said below
- middle_transfer: float32 [128, 64, 64], P('leaf'), may hold values from -0.5 to 0.5
- middle_coupling: float32 [192, 4, 64, 64], P('leaf'), may hold values from -0.75 to 0.75
- middle_lists: int32 [192, 4], P('leaf'), may hold values from -1 to 127, as said below
- upper_transfer: float32 [126, 64, 64], replicated, may hold values from -0.5 to 0.5
- upper_coupling: float32 [64, 4, 64, 64], P('leaf'), may hold values from -1 to 1
- upper_lists: int32 [64, 4], P('leaf'), may hold values from -1 to 31, as said below
Outputs:
- first_product: float32 [8, 1024, 256], P(None, ('leaf', 'rhs'))
- second_product: float32 [8, 1024, 256], P(None, ('leaf', 'rhs'))
Inputs may be any that keep to these rules, and one draw needn't show every extreme that they name: `near_pairs`: each slot holds (receiving leaf, source leaf). The 32 slots of each device along leaf+rhs belong to receiving leaves among that device's 4 leaves; live pairs come first, the remaining slots are -1 in both columns. The source leaf lies within 4 leaves of the receiving one. In every draw some device has all its slots live. `local_lists`: each entry is -1 (unused) or the number, among the clusters of the same level counted from 0 in leaf order, of a cluster whose number differs from the listing cluster's by 2 or 3; entries of one list differ. `middle_lists`: as for the local lists, at the level of the subtree roots and the level below it. `upper_lists`: row h lists for heap cluster h (level t with 2^t <= h < 2^(t+1), number h - 2^t) as for the local lists; rows 0 to 3 are -1.
All inputs are finite; a program needn't handle non-finite values.
Results may differ from a plain program's by a relative error of at most 0.0003.
Values sent between devices are 32-bit elements; how exact they have to be, the bound alone decides.
A program may use at most 128 MiB of HBM per device.

v0:
```python
import jax
import jax.numpy as jnp
from jax import lax
from jax.sharding import PartitionSpec as P

NEAR_REACH = 4
highest = lax.Precision.HIGHEST


def with_halo(shard, sides, width):
    for axis, dim in sides:
        count, length = (lax.axis_size(axis), shard.shape[dim])
        up = [(i, (i + 1) % count) for i in range(count - 1)]
        down = [(j, i) for i, j in up]
        last = lax.slice_in_dim(shard, length - width, length, axis=dim)
        leading = lax.slice_in_dim(shard, 0, width, axis=dim)
        before = lax.ppermute(last, axis, up)
        after = lax.ppermute(leading, axis, down)
        shard = jnp.concatenate([before, shard, after], axis=dim)
    return shard


def lift_level(matrices, vectors):
    moved = jnp.einsum("nab,cna->cnb", matrices, vectors, precision=highest)
    return moved.reshape(moved.shape[0], moved.shape[1] // 2, 2, moved.shape[2]).sum(axis=2)


def couple_lists(blocks, positions, valid, table):
    clipped = jnp.clip(positions, 0, table.shape[1] - 1)
    picked = jnp.take(table, clipped, axis=1)
    picked = picked * valid.astype(table.dtype)[None, :, :, None]
    return jnp.einsum("nkab,cnkb->cna", blocks, picked, precision=highest)


def near_field(vectors_rows, near_blocks, near_pairs, first_leaf):
    extended = with_halo(vectors_rows, ((("leaf", "rhs"), 1),), NEAR_REACH)
    leaf_share = vectors_rows.shape[1]
    sources = jnp.clip(near_pairs[:, 1] - first_leaf + NEAR_REACH, 0, extended.shape[1] - 1)
    picked = jnp.take(extended, sources, axis=1)
    terms = jnp.einsum("pij,rpj->rpi", near_blocks, picked, precision=highest)
    targets = near_pairs[:, 0] - first_leaf
    owners = (targets[None, :] == jnp.arange(leaf_share, dtype=jnp.int32)[:, None]).astype(
        jnp.float32
    )
    return jnp.einsum("lp,rpi->rli", owners, terms, precision=highest)


def tree_pass(leaf_coeffs, group, groups, tree_data):
    (
        local_transfer,
        local_coupling,
        local_lists,
        middle_transfer,
        middle_coupling,
        middle_lists,
        upper_transfer,
        upper_coupling,
        upper_lists,
    ) = tree_data
    leaf_total = leaf_coeffs.shape[1]
    local_levels = leaf_total.bit_length() - 2
    top_depth = groups.bit_length() - 1
    amounts = [4 * 2**sublevel for sublevel in range(local_levels)]
    offsets = [4 * (2**sublevel - 1) for sublevel in range(local_levels)]
    upward = [leaf_coeffs] * local_levels
    for sublevel in range(local_levels - 1, 0, -1):
        start_row = offsets[sublevel]
        upward[sublevel - 1] = lift_level(
            local_transfer[start_row : start_row + amounts[sublevel]], upward[sublevel]
        )
    upper_pair = lift_level(local_transfer[0:4], upward[0])
    subtree_root = lift_level(middle_transfer, upper_pair)
    rims = jnp.stack(
        [
            jnp.concatenate([level_coeffs[:, :3], level_coeffs[:, -3:]], axis=1)
            for level_coeffs in upward
        ],
        axis=1,
    )
    bordered = with_halo(rims, (("leaf", 2),), 3)
    all_roots, all_pairs = (
        lax.all_gather(subtree_root, "leaf", axis=1, tiled=True),
        lax.all_gather(upper_pair, "leaf", axis=1, tiled=True),
    )
    climbing = {top_depth: all_roots}
    for tree_level in range(top_depth, 0, -1):
        lower_end = 2**tree_level
        climbing[tree_level - 1] = lift_level(
            upper_transfer[lower_end - 2 : 2 * lower_end - 2], climbing[tree_level]
        )
    numbered = jnp.concatenate(
        [jnp.zeros_like(climbing[0])] + [climbing[tree_level] for tree_level in range(top_depth)],
        axis=1,
    )
    level_start = jnp.int32(1)
    for exponent in range(1, top_depth):
        level_start = jnp.where(group >= 2**exponent, 2**exponent, level_start)
    owned_terms = couple_lists(
        upper_coupling, upper_lists + level_start, upper_lists >= 0, numbered
    )
    ancestor = lax.all_gather(owned_terms, "leaf", axis=1, tiled=True)
    descending = jnp.zeros_like(owned_terms[:, 0])
    for tree_level in range(1, top_depth):
        node_index = 2**tree_level + group // 2 ** (top_depth - tree_level)
        matrix = lax.dynamic_index_in_dim(upper_transfer, node_index - 2, 0, keepdims=False)
        descending = lax.dynamic_index_in_dim(ancestor, node_index, 1, keepdims=False) + jnp.einsum(
            "ab,cb->ca", matrix, descending, precision=highest
        )
    root_matrix = lax.dynamic_index_in_dim(upper_transfer, groups - 2 + group, 0, keepdims=False)
    root_lists = middle_lists[0:1]
    root_down = couple_lists(middle_coupling[0:1], root_lists, root_lists >= 0, all_roots)[
        :, 0
    ] + jnp.einsum("ab,cb->ca", root_matrix, descending, precision=highest)
    pair_lists = middle_lists[1:3]
    descending = couple_lists(
        middle_coupling[1:3], pair_lists, pair_lists >= 0, all_pairs
    ) + jnp.einsum("nab,cb->cna", middle_transfer, root_down, precision=highest)
    for sublevel in range(local_levels):
        amount = amounts[sublevel]
        offset = offsets[sublevel]
        extended = jnp.concatenate(
            [bordered[:, sublevel, :3], upward[sublevel], bordered[:, sublevel, 9:]], axis=1
        )
        entries = local_lists[offset : offset + amount]
        coupled = couple_lists(
            local_coupling[offset : offset + amount],
            entries - group * amount + 3,
            entries >= 0,
            extended,
        )
        descending = coupled + jnp.einsum(
            "nab,cnb->cna",
            local_transfer[offset : offset + amount],
            jnp.repeat(descending, 2, axis=1),
            precision=highest,
        )
    return descending


def apply_matrix(vectors_rows, near_blocks, near_pairs, leaf_basis, tree_data):
    group = lax.axis_index("leaf")
    groups = lax.axis_size("leaf")
    quarter = lax.axis_index("rhs")
    quarters = lax.axis_size("rhs")
    leaf_share = vectors_rows.shape[1]
    first_leaf = (group * quarters + quarter) * leaf_share
    near_part = near_field(vectors_rows, near_blocks, near_pairs, first_leaf)
    own_coeffs = jnp.einsum("lki,rli->rlk", leaf_basis, vectors_rows, precision=highest)
    leaf_coeffs = lax.all_gather(own_coeffs, "rhs", axis=1, tiled=True)
    descending = tree_pass(leaf_coeffs, group, groups, tree_data)
    own_rows = lax.dynamic_slice_in_dim(descending, quarter * leaf_share, leaf_share, 1)
    far_part = jnp.einsum("lki,rlk->rli", leaf_basis, own_rows, precision=highest)
    return near_part + far_part


def body(
    input_columns,
    near_blocks,
    near_pairs,
    leaf_basis,
    local_transfer,
    local_coupling,
    local_lists,
    middle_transfer,
    middle_coupling,
    middle_lists,
    upper_transfer,
    upper_coupling,
    upper_lists,
):
    tree_data = (
        local_transfer,
        local_coupling,
        local_lists,
        middle_transfer,
        middle_coupling,
        middle_lists,
        upper_transfer,
        upper_coupling,
        upper_lists,
    )
    vectors_rows = lax.all_to_all(input_columns, "rhs", split_axis=1, concat_axis=0, tiled=True)
    first_product = apply_matrix(vectors_rows, near_blocks, near_pairs, leaf_basis, tree_data)
    second_product = apply_matrix(first_product, near_blocks, near_pairs, leaf_basis, tree_data)
    return (first_product, second_product)


def solution(mesh):
    in_specs = (
        P("rhs", "leaf", None),
        P(("leaf", "rhs"), None, None),
        P(("leaf", "rhs"), None),
        P(("leaf", "rhs"), None, None),
        P("leaf", None, None),
        P("leaf", None, None, None),
        P("leaf", None),
        P("leaf", None, None),
        P("leaf", None, None, None),
        P("leaf", None),
        P(),
        P("leaf", None, None, None),
        P("leaf", None),
    )
    out_specs = (P(None, ("leaf", "rhs"), None), P(None, ("leaf", "rhs"), None))
    return jax.shard_map(body, mesh=mesh, in_specs=in_specs, out_specs=out_specs, check_vma=False)
```

profile of v0, /device:TPU:1, one launch (start us, length us, event | category | flops | bytes accessed | tf_op | source)
XLA Modules:
  0.0 549.1 jit_solution(10016394474385720229)
XLA Ops:
  0.6 1.4 copy.124
  2.1 5.0 all-to-all-start
  15.4 13.1 %constant_dynamic-slice_fusion.5 = (f32[1,64,64]{0,2,1:T(8,128)}, f32[1,64,64]{0,2,1:T(8,128)}, f32[1,64,64]{0,2,1:T(8,128)}, f32[1,64,64]{0,2,1:T(8,128)}, f32[1,64,64]{0,2,1:T(8,128)}, /*index=5*/f32[1,64,64]{0,2,1:T(8,128)}) fusion(f32[126,64,64]{0,2,1:T(8,128)} %param.35, s32[]{:T(128)S(6)} %select_n.163, s32[]{:T(128)S(6)} %select_n.162, ...), kind=kLoop, calls=%fused_computation.260 | loop fusion | bytes 196632 | tf_op jit(solution)/shard_map/jit(dynamic_index_in_dim)/dynamic_slice | solution.py:109
  28.5 2.4 copy.181
  36.4 2.0 slice.203
  38.4 1.9 slice.204
  40.3 1.9 slice.205
  42.2 1.9 slice.206
  44.2 1.9 slice.207
  46.1 4.3 copy.175
  50.4 3.4 copy.176
  53.7 3.0 copy.177
  56.8 2.2 copy.178
  59.0 2.9 copy.179
  63.2 3.0 copy.182
  67.5 3.0 copy.184
  70.6 2.9 copy.185
  82.6 9.6 %all_gather.24 = f32[8,16,64]{2,0,1:T(8,128)S(1)} all-gather(f32[8,4,64]{2,0,1:T(8,128)S(1)} %convolution_bitcast_fusion.7), channel_id=1, replica_groups=mesh['leaf'=64,'rhs'=4] {'rhs'}, dimensions={1}, use_global_device_ids=true | all-gather | bytes 40960 | tf_op jit(solution)/shard_map/all_gather | solution.py:149
  95.1 3.1 collective-permute-start
  98.2 7.9 %collective-permute-start.1 = (f32[8,4,256]{2,0,1:T(8,128)}, f32[8,4,256]{2,0,1:T(8,128)}, u32[]{:S(2)}, u32[]{:S(2)}) collective-permute-start(f32[8,4,256]{2,0,1:T(8,128)} %all_to_all.16), channel_id=1, source_target_pairs={{1,0},{2,1},{3,2},{4,3},{5,4},{6,5},{7,6},{8,7},{9,8},{10,9},{11,1... | collective-permute-start | bytes 98312 | tf_op jit(solution)/shard_map/ppermute | solution.py:18
  106.2 58.5 %all_gather.25 = f32[8,128,64]{2,0,1:T(8,128)} all-gather(f32[8,2,64]{2,0,1:T(8,128)S(1)} %bitcast_reduce_fusion.15), channel_id=1, replica_groups=mesh['leaf'=64,'rhs'=4] {'leaf'}, dimensions={1}, use_global_device_ids=true | all-gather | bytes 266240 | tf_op jit(solution)/shard_map/all_gather | solution.py:83
  165.8 43.2 %all-gather.4 = f32[64,64,8]{1,2,0:T(8,128)S(1)} all-gather(f32[1,64,8]{1,2,0:T(8,128)S(1)} %convolution_bitcast_fusion.19), channel_id=2, replica_groups=mesh['leaf'=64,'rhs'=4] {'leaf'}, dimensions={0}, use_global_device_ids=true | all-gather | bytes 133120 | tf_op jit(solution)/shard_map/all_gather | solution.py:82
  209.7 1.7 reshape.343
  211.4 1.7 reshape.316
  213.2 1.9 copy.137
  215.1 2.9 bitcast_reduce_fusion.1
  221.0 2.2 gather_fusion.6
  224.4 42.1 %all-gather.5 = f32[64,64,8]{1,2,0:T(8,128)S(1)} all-gather(f32[1,64,8]{1,2,0:T(8,128)S(1)} %convolution_bitcast_fusion.16), channel_id=3, replica_groups=mesh['leaf'=64,'rhs'=4] {'leaf'}, dimensions={0}, use_global_device_ids=true | all-gather | bytes 133120 | tf_op jit(solution)/shard_map/all_gather | solution.py:101
  267.2 1.7 reshape.345
  268.9 1.7 reshape.317
  272.8 2.5 collective-permute-start.2
  275.3 2.6 collective-permute-start.3
  277.9 2.2 gather_fusion.5
  280.1 2.3 gather_fusion.4
  289.1 1.4 convolution_bitcast_fusion.11
  290.5 1.7 convolution_add_fusion.5
  295.5 2.1 gather_fusion.3
  297.6 1.7 convolution_bitcast_fusion.9
  300.9 1.4 pad_maximum_fusion.6
  302.3 2.2 gather_fusion.2
  304.5 2.3 convolution_bitcast_fusion.4
  308.1 1.6 fusion.28
  310.3 2.3 gather_fusion.1
  312.6 3.6 fusion.4
  316.2 1.6 fusion.106
  317.8 1.4 pad_maximum_fusion.1
  319.2 2.3 gather_fusion
  321.5 10.5 %convolution_bitcast_fusion.1 = f32[8,32,256]{2,0,1:T(8,128)S(1)} fusion(f32[32,256,256]{2,1,0:T(8,128)} %param.26, f32[32,8,256]{2,1,0:T(8,128)} %gather_fusion, pred[32]{0:T(512)(128)(4,1)S(1)} %copy-done.55), kind=kOutput, calls=%fused_computation.19 | convolution fusion | flops 201392128 | bytes 8912928 | tf_op jit(solution)/shard_map/pij,rpj->rpi/dot_general | solution.py:40
  333.9 9.6 %all_gather.28 = f32[8,16,64]{2,0,1:T(8,128)S(1)} all-gather(f32[8,4,64]{2,0,1:T(8,128)S(1)} %convolution_bitcast_fusion.6), channel_id=1, replica_groups=mesh['leaf'=64,'rhs'=4] {'rhs'}, dimensions={1}, use_global_device_ids=true | all-gather | bytes 40960 | tf_op jit(solution)/shard_map/all_gather | solution.py:149
  347.2 48.4 %all-gather.6 = f32[64,64,8]{1,2,0:T(8,128)S(1)} all-gather(f32[1,64,8]{1,2,0:T(8,128)S(1)} %convolution_bitcast_fusion.15), channel_id=4, replica_groups=mesh['leaf'=64,'rhs'=4] {'leaf'}, dimensions={0}, use_global_device_ids=true | all-gather | bytes 133120 | tf_op jit(solution)/shard_map/all_gather | solution.py:82
  396.3 1.7 reshape.347
  398.1 1.7 reshape.318
  399.8 2.9 bitcast_reduce_fusion
  403.0 47.4 %all_gather.29 = f32[8,128,64]{2,0,1:T(8,128)S(1)} all-gather(f32[8,2,64]{2,0,1:T(8,128)S(1)} %copy-done.37), channel_id=1, replica_groups=mesh['leaf'=64,'rhs'=4] {'leaf'}, dimensions={1}, use_global_device_ids=true | all-gather | bytes 266240 | tf_op jit(solution)/shard_map/all_gather | solution.py:83
  450.4 1.9 collective-permute-start.4
  452.3 4.9 collective-permute-start.5
  457.3 4.3 collective-permute-start.6
  461.6 2.1 collective-permute-start.7
  469.7 1.6 gather_fusion.13
  472.3 48.5 %all-gather.7 = f32[64,64,8]{1,2,0:T(8,128)S(1)} all-gather(f32[1,64,8]{1,2,0:T(8,128)S(1)} %convolution_bitcast_fusion.12), channel_id=5, replica_groups=mesh['leaf'=64,'rhs'=4] {'leaf'}, dimensions={0}, use_global_device_ids=true | all-gather | bytes 133120 | tf_op jit(solution)/shard_map/all_gather | solution.py:101
  526.4 3.5 fusion.7
  530.5 1.6 convolution_bitcast_fusion.8
  532.8 2.2 convolution_bitcast_fusion.2
  538.7 9.3 %convolution_bitcast_fusion = f32[8,32,256]{2,0,1:T(8,128)S(1)} fusion(f32[32,256,256]{2,1,0:T(8,128)} %param.26, f32[32,8,256]{2,1,0:T(8,128)S(1)} %gather_fusion.7, pred[32]{0:T(512)(128)(4,1)S(1)} %copy-done.56), kind=kOutput, calls=%fused_computation.18 | convolution fusion | flops 201392128 | bytes 8912928 | tf_op jit(solution)/shard_map/pij,rpj->rpi/dot_general | solution.py:40
  (273 shorter events, 75.5 us)
Async XLA Ops:
  0.6 80.8 %copy-start = (f32[4,64,256]{2,1,0:T(8,128)S(1)}, f32[4,64,256]{2,1,0:T(8,128)}, u32[]{:S(2)}) copy-start(f32[4,64,256]{2,1,0:T(8,128)} %param.28) | copy-start | bytes 786436
  2.1 77.9 %all-to-all-start = ((f32[2,16,256]{2,0,1:T(2,128)}), f32[2,16,256]{2,0,1:T(2,128)}, u32[]{:S(2)}, u32[]{:S(2)}) async-start(f32[2,16,256]{2,0,1:T(2,128)} %copy.124), calls=%async_computation | async-start | bytes 65536 | tf_op jit(solution)/shard_map/all_to_all | solution.py:182
  28.5 5.5 %copy-start.63 = (s32[1,4]{1,0:T(1,128)S(1)}, s32[1,4]{1,0:T(1,128)}, u32[]{:S(2)}) copy-start(s32[1,4]{1,0:T(1,128)} %param.37) | copy-start | bytes 52
  28.5 7.9 %copy-start.1 = (f32[126,64,64]{0,2,1:T(8,128)S(1)}, f32[126,64,64]{0,2,1:T(8,128)}, u32[]{:S(2)}) copy-start(f32[126,64,64]{0,2,1:T(8,128)} %param.35) | copy-start | bytes 6193156
  67.5 6.0 %copy-start.6 = (f32[1,64,64]{0,2,1:T(8,128)S(1)}, f32[1,64,64]{0,2,1:T(8,128)}, u32[]{:S(2)}) copy-start(f32[1,64,64]{0,2,1:T(8,128)} %get-tuple-element.20) | copy-start | bytes 49156
  70.6 21.6 %copy-start.3 = (f32[28,64,64]{2,1,0:T(8,128)S(1)}, f32[28,64,64]{2,1,0:T(8,128)}, u32[]{:S(2)}) copy-start(f32[28,64,64]{2,1,0:T(8,128)} %param.29) | copy-start | bytes 1376260
  81.4 133.6 %copy-start.2 = (f32[64,64,64]{2,1,0:T(8,128)S(1)}, f32[64,64,64]{2,1,0:T(8,128)}, u32[]{:S(2)}) copy-start(f32[64,64,64]{2,1,0:T(8,128)} %copy.175) | copy-start | bytes 3145732
  92.2 72.5 %copy-start.16 = (f32[8,16,64]{2,0,1:T(8,128)}, f32[8,16,64]{2,0,1:T(8,128)S(1)}, u32[]{:S(2)}) copy-start(f32[8,16,64]{2,0,1:T(8,128)S(1)} %all_gather.24) | copy-start | bytes 98308
  92.7 72.0 %copy-start.25 = (f32[8,8,64]{2,0,1:T(8,128)}, f32[8,8,64]{2,0,1:T(8,128)S(1)}, u32[]{:S(2)}) copy-start(f32[8,8,64]{2,0,1:T(8,128)S(1)} %bitcast_reduce_fusion.7) | copy-start | bytes 49156
  95.1 222.6 %collective-permute-start = (f32[8,4,256]{2,0,1:T(8,128)}, f32[8,4,256]{2,0,1:T(8,128)}, u32[]{:S(2)}, u32[]{:S(2)}) collective-permute-start(f32[8,4,256]{2,0,1:T(8,128)} %all_to_all.16), channel_id=1, source_target_pairs={{0,1},{1,2},{2,3},{3,4},{4,5},{5,6},{6,7},{7,8},{8,9},{9,10},{10,1... | collective-permute-start | bytes 98312 | tf_op jit(solution)/shard_map/ppermute | solution.py:17
  98.2 219.5 %collective-permute-start.1 = (f32[8,4,256]{2,0,1:T(8,128)}, f32[8,4,256]{2,0,1:T(8,128)}, u32[]{:S(2)}, u32[]{:S(2)}) collective-permute-start(f32[8,4,256]{2,0,1:T(8,128)} %all_to_all.16), channel_id=1, source_target_pairs={{1,0},{2,1},{3,2},{4,3},{5,4},{6,5},{7,6},{8,7},{9,8},{10,9},{11,1... | collective-permute-start | bytes 98312 | tf_op jit(solution)/shard_map/ppermute | solution.py:18
  213.1 4.8 copy-start.4
  213.1 5.8 %copy-start.8 = (f32[16,64,64]{2,1,0:T(8,128)S(1)}, f32[16,64,64]{2,1,0:T(8,128)}, u32[]{:S(2)}) copy-start(f32[16,64,64]{2,1,0:T(8,128)} %copy.177) | copy-start | bytes 786436
  215.1 4.9 copy-start.20
  215.1 4.9 copy-start.61
  272.8 19.5 %collective-permute-start.2 = (f32[8,3,3,64]{3,0,2,1:T(8,128)}, f32[8,3,3,64]{3,0,2,1:T(8,128)}, u32[]{:S(2)}, u32[]{:S(2)}) collective-permute-start(f32[8,3,3,64]{3,0,2,1:T(8,128)} %get-tuple-element.38), channel_id=1, source_target_pairs={{0,4},{4,8},{8,12},{12,16},{16,20},{20,24},{24,28},{28,32},{32,36}... | collective-permute-start | bytes 55304 | tf_op jit(solution)/shard_map/ppermute | solution.py:17
  275.3 18.3 %collective-permute-start.3 = (f32[8,3,3,64]{3,0,2,1:T(8,128)}, f32[8,3,3,64]{3,0,2,1:T(8,128)}, u32[]{:S(2)}, u32[]{:S(2)}) collective-permute-start(f32[8,3,3,64]{3,0,2,1:T(8,128)} %get-tuple-element.39), channel_id=1, source_target_pairs={{4,0},{8,4},{12,8},{16,12},{20,16},{24,20},{28,24},{32,28},{36,32}... | collective-permute-start | bytes 55304 | tf_op jit(solution)/shard_map/ppermute | solution.py:18
  297.6 15.0 %copy-start.34 = (f32[16,4]{1,0:T(8,128)S(1)}, f32[16,4]{1,0:T(8,128)}, u32[]{:S(2)}) copy-start(f32[16,4]{1,0:T(8,128)} %copy.129) | copy-start | bytes 772
  297.6 15.0 %copy-start.51 = (pred[16,4]{1,0:T(8,128)(4,1)S(1)}, pred[16,4]{1,0:T(8,128)(4,1)}, u32[]{:S(2)}) copy-start(pred[16,4]{1,0:T(8,128)(4,1)} %copy.127) | copy-start | bytes 196
  304.5 5.2 copy-start.17
  304.5 5.2 copy-start.38
  304.5 5.2 copy-start.39
  309.6 11.8 %copy-start.55 = (pred[32]{0:T(512)(128)(4,1)S(1)}, pred[32]{0:T(512)(128)(4,1)}, u32[]{:S(2)}) copy-start(pred[32]{0:T(512)(128)(4,1)} %get-tuple-element.18) | copy-start | bytes 100
  312.6 5.2 copy-start.31
  321.5 10.5 %copy-start.32 = (f32[4,8,256]{2,1,0:T(8,128)S(1)}, f32[4,8,256]{2,1,0:T(8,128)}, u32[]{:S(2)}) copy-start(f32[4,8,256]{2,1,0:T(8,128)} %fusion.106) | copy-start | bytes 98308
  321.5 10.5 %copy-start.58 = (s32[32]{0:T(128)S(1)}, s32[32]{0:T(128)}, u32[]{:S(2)}) copy-start(s32[32]{0:T(128)} %subtract_bitcast_fusion) | copy-start | bytes 388
  321.5 25.5 %copy-start.14 = (f32[2,64,64]{2,1,0:T(8,128)S(1)}, f32[2,64,64]{2,1,0:T(8,128)}, u32[]{:S(2)}) copy-start(f32[2,64,64]{2,1,0:T(8,128)} %param.32) | copy-start | bytes 98308
  399.8 57.4 %copy-start.44 = (f32[8,3,64]{2,0,1:T(8,128)S(1)}, f32[8,3,64]{2,0,1:T(8,128)}, u32[]{:S(2)}) copy-start(f32[8,3,64]{2,0,1:T(8,128)} %get-tuple-element.60) | copy-start | bytes 18436
  399.8 57.4 %copy-start.45 = (f32[8,3,64]{2,0,1:T(8,128)S(1)}, f32[8,3,64]{2,0,1:T(8,128)}, u32[]{:S(2)}) copy-start(f32[8,3,64]{2,0,1:T(8,128)} %get-tuple-element.61) | copy-start | bytes 18436
  399.8 57.4 %copy-start.42 = (f32[8,3,64]{2,0,1:T(8,128)S(1)}, f32[8,3,64]{2,0,1:T(8,128)}, u32[]{:S(2)}) copy-start(f32[8,3,64]{2,0,1:T(8,128)} %get-tuple-element.56) | copy-start | bytes 18436
  399.8 57.4 %copy-start.43 = (f32[8,3,64]{2,0,1:T(8,128)S(1)}, f32[8,3,64]{2,0,1:T(8,128)}, u32[]{:S(2)}) copy-start(f32[8,3,64]{2,0,1:T(8,128)} %get-tuple-element.57) | copy-start | bytes 18436
  399.8 57.5 %copy-start.40 = (f32[8,3,64]{2,0,1:T(8,128)S(1)}, f32[8,3,64]{2,0,1:T(8,128)}, u32[]{:S(2)}) copy-start(f32[8,3,64]{2,0,1:T(8,128)} %get-tuple-element.40) | copy-start | bytes 18436
  399.8 57.5 %copy-start.41 = (f32[8,3,64]{2,0,1:T(8,128)S(1)}, f32[8,3,64]{2,0,1:T(8,128)}, u32[]{:S(2)}) copy-start(f32[8,3,64]{2,0,1:T(8,128)} %get-tuple-element.41) | copy-start | bytes 18436
  399.8 63.9 %copy-start.5 = (f32[32,64,64]{2,1,0:T(8,128)S(1)}, f32[32,64,64]{2,1,0:T(8,128)}, u32[]{:S(2)}) copy-start(f32[32,64,64]{2,1,0:T(8,128)} %copy.176) | copy-start | bytes 1572868
  399.8 64.8 %copy-start.9 = (f32[16,64,64]{2,1,0:T(8,128)S(1)}, f32[16,64,64]{2,1,0:T(8,128)}, u32[]{:S(2)}) copy-start(f32[16,64,64]{2,1,0:T(8,128)} %copy.177) | copy-start | bytes 786436
  402.8 62.8 %copy-start.13 = (f32[4,64,64]{2,1,0:T(8,128)S(1)}, f32[4,64,64]{2,1,0:T(8,128)}, u32[]{:S(2)}) copy-start(f32[4,64,64]{2,1,0:T(8,128)} %copy.179) | copy-start | bytes 196612
  402.8 63.0 %copy-start.21 = (f32[2,64,64]{2,1,0:T(8,128)S(1)}, f32[2,64,64]{2,1,0:T(8,128)}, u32[]{:S(2)}) copy-start(f32[2,64,64]{2,1,0:T(8,128)} %copy.180) | copy-start | bytes 98308
  403.0 68.4 %copy-start.22 = (f32[1,4,64,64]{3,2,1,0:T(8,128)S(1)}, f32[1,4,64,64]{3,2,1,0:T(8,128)}, u32[]{:S(2)}) copy-start(f32[1,4,64,64]{3,2,1,0:T(8,128)} %param.36) | copy-start | bytes 196612
  450.4 86.7 %collective-permute-start.4 = (f32[8,4,256]{2,1,0:T(4,128)}, f32[8,4,256]{2,1,0:T(4,128)}, u32[]{:S(2)}, u32[]{:S(2)}) collective-permute-start(f32[8,4,256]{2,1,0:T(4,128)} %fusion.13), channel_id=1, source_target_pairs={{0,1},{1,2},{2,3},{3,4},{4,5},{5,6},{6,7},{7,8},{8,9},{9,10},{10,1... | collective-permute-start | bytes 98312 | tf_op jit(solution)/shard_map/ppermute | solution.py:17
  452.3 84.8 %collective-permute-start.5 = (f32[8,4,256]{2,1,0:T(4,128)}, f32[8,4,256]{2,1,0:T(4,128)}, u32[]{:S(2)}, u32[]{:S(2)}) collective-permute-start(f32[8,4,256]{2,1,0:T(4,128)} %fusion.13), channel_id=1, source_target_pairs={{1,0},{2,1},{3,2},{4,3},{5,4},{6,5},{7,6},{8,7},{9,8},{10,9},{11,1... | collective-permute-start | bytes 98312 | tf_op jit(solution)/shard_map/ppermute | solution.py:18
  457.3 68.3 %collective-permute-start.6 = (f32[8,3,3,64]{3,0,2,1:T(8,128)S(1)}, f32[8,3,3,64]{3,0,2,1:T(8,128)S(1)}, u32[]{:S(2)}, u32[]{:S(2)}) collective-permute-start(f32[8,3,3,64]{3,0,2,1:T(8,128)S(1)} %get-tuple-element.36), channel_id=1, source_target_pairs={{0,4},{4,8},{8,12},{12,16},{16,20},{20,24},{24,28},{28,32},{32,36}... | collective-permute-start | bytes 55304 | tf_op jit(solution)/shard_map/ppermute | solution.py:17
  461.6 60.1 %copy-start.11 = (f32[3,4,64,64]{3,2,1,0:T(8,128)S(1)}, f32[3,4,64,64]{3,2,1,0:T(8,128)}, u32[]{:S(2)}) copy-start(f32[3,4,64,64]{3,2,1,0:T(8,128)} %param.33) | copy-start | bytes 589828
  461.6 64.1 %collective-permute-start.7 = (f32[8,3,3,64]{3,0,2,1:T(8,128)S(1)}, f32[8,3,3,64]{3,0,2,1:T(8,128)S(1)}, u32[]{:S(2)}, u32[]{:S(2)}) collective-permute-start(f32[8,3,3,64]{3,0,2,1:T(8,128)S(1)} %get-tuple-element.37), channel_id=1, source_target_pairs={{4,0},{8,4},{12,8},{16,12},{20,16},{24,20},{28,24},{32,28},{36,32}... | collective-permute-start | bytes 55304 | tf_op jit(solution)/shard_map/ppermute | solution.py:18
  464.7 58.8 %copy-start.54 = (f32[2,4]{1,0:T(2,128)S(1)}, f32[2,4]{1,0:T(2,128)}, u32[]{:S(2)}) copy-start(f32[2,4]{1,0:T(2,128)} %get-tuple-element.67) | copy-start | bytes 100
  464.7 59.8 %copy-start.30 = (f32[1,64,64]{2,1,0:T(8,128)S(1)}, f32[1,64,64]{2,1,0:T(8,128)}, u32[]{:S(2)}) copy-start(f32[1,64,64]{2,1,0:T(8,128)} %copy.182) | copy-start | bytes 49156
  464.7 59.8 %copy-start.48 = (f32[8,64]{1,0:T(8,128)S(1)}, f32[8,64]{1,0:T(8,128)}, u32[]{:S(2)}) copy-start(f32[8,64]{1,0:T(8,128)} %fusion.90) | copy-start | bytes 6148
  464.7 59.9 %copy-start.29 = (f32[1,64,64]{2,1,0:T(8,128)S(1)}, f32[1,64,64]{2,1,0:T(8,128)}, u32[]{:S(2)}) copy-start(f32[1,64,64]{2,1,0:T(8,128)} %copy.183) | copy-start | bytes 49156
  464.7 60.1 %copy-start.28 = (f32[1,64,64]{2,1,0:T(8,128)S(1)}, f32[1,64,64]{2,1,0:T(8,128)}, u32[]{:S(2)}) copy-start(f32[1,64,64]{2,1,0:T(8,128)} %copy.184) | copy-start | bytes 49156
  464.7 60.3 %copy-start.27 = (f32[1,64,64]{2,1,0:T(8,128)S(1)}, f32[1,64,64]{2,1,0:T(8,128)}, u32[]{:S(2)}) copy-start(f32[1,64,64]{2,1,0:T(8,128)} %copy.185) | copy-start | bytes 49156
  464.7 60.4 %copy-start.26 = (f32[1,64,64]{2,1,0:T(8,128)S(1)}, f32[1,64,64]{2,1,0:T(8,128)}, u32[]{:S(2)}) copy-start(f32[1,64,64]{2,1,0:T(8,128)} %copy.186) | copy-start | bytes 49156
  464.7 60.6 %copy-start.15 = (f32[2,64,64]{2,1,0:T(8,128)S(1)}, f32[2,64,64]{2,1,0:T(8,128)}, u32[]{:S(2)}) copy-start(f32[2,64,64]{2,1,0:T(8,128)} %param.32) | copy-start | bytes 98308
  465.3 60.4 %copy-start.19 = (f32[8,16,64]{2,0,1:T(8,128)S(1)}, f32[8,16,64]{2,0,1:T(8,128)}, u32[]{:S(2)}) copy-start(f32[8,16,64]{2,0,1:T(8,128)} %copy-done.18) | copy-start | bytes 98308
  465.3 60.5 %copy-start.33 = (s32[1024]{0:T(1024)S(1)}, s32[1024]{0:T(1024)}, u32[]{:S(2)}) copy-start(s32[1024]{0:T(1024)} %get-tuple-element.74) | copy-start | bytes 12292
  465.8 60.6 %copy-start.35 = (f32[16,4]{1,0:T(8,128)S(1)}, f32[16,4]{1,0:T(8,128)}, u32[]{:S(2)}) copy-start(f32[16,4]{1,0:T(8,128)} %copy.129) | copy-start | bytes 772
  465.8 60.6 %copy-start.52 = (pred[16,4]{1,0:T(8,128)(4,1)S(1)}, pred[16,4]{1,0:T(8,128)(4,1)}, u32[]{:S(2)}) copy-start(pred[16,4]{1,0:T(8,128)(4,1)} %copy.127) | copy-start | bytes 196
  521.8 8.2 %copy-start.53 = (s32[1024]{0:T(1024)S(1)}, s32[1024]{0:T(1024)}, u32[]{:S(2)}) copy-start(s32[1024]{0:T(1024)} %get-tuple-element.72) | copy-start | bytes 12292
  523.4 7.1 %copy-start.49 = (f32[4,4]{1,0:T(4,128)S(1)}, f32[4,4]{1,0:T(4,128)}, u32[]{:S(2)}) copy-start(f32[4,4]{1,0:T(4,128)} %copy.135) | copy-start | bytes 196
  523.4 7.1 %copy-start.60 = (pred[4,4]{1,0:T(4,128)(4,1)S(1)}, pred[4,4]{1,0:T(4,128)(4,1)}, u32[]{:S(2)}) copy-start(pred[4,4]{1,0:T(4,128)(4,1)} %copy.133) | copy-start | bytes 52
  525.4 6.8 %copy-start.24 = (f32[8,8,64]{2,0,1:T(8,128)S(1)}, f32[8,8,64]{2,0,1:T(8,128)}, u32[]{:S(2)}) copy-start(f32[8,8,64]{2,0,1:T(8,128)} %copy-done.23) | copy-start | bytes 49156
  525.7 6.5 %copy-start.46 = (s32[1024]{0:T(1024)S(1)}, s32[1024]{0:T(1024)}, u32[]{:S(2)}) copy-start(s32[1024]{0:T(1024)} %get-tuple-element.73) | copy-start | bytes 12292
  525.8 7.0 %copy-start.47 = (f32[8,4]{1,0:T(8,128)S(1)}, f32[8,4]{1,0:T(8,128)}, u32[]{:S(2)}) copy-start(f32[8,4]{1,0:T(8,128)} %copy.132) | copy-start | bytes 388
  525.8 7.0 %copy-start.57 = (pred[8,4]{1,0:T(8,128)(4,1)S(1)}, pred[8,4]{1,0:T(8,128)(4,1)}, u32[]{:S(2)}) copy-start(pred[8,4]{1,0:T(8,128)(4,1)} %copy.130) | copy-start | bytes 100
  532.2 6.6 %copy-start.56 = (pred[32]{0:T(512)(128)(4,1)S(1)}, pred[32]{0:T(512)(128)(4,1)}, u32[]{:S(2)}) copy-start(pred[32]{0:T(512)(128)(4,1)} %get-tuple-element.18) | copy-start | bytes 100
  538.7 9.3 %copy-start.59 = (s32[32]{0:T(128)S(1)}, s32[32]{0:T(128)}, u32[]{:S(2)}) copy-start(s32[32]{0:T(128)} %subtract_bitcast_fusion) | copy-start | bytes 388
  (9 other events, 25.0 us)
where the time goes:
time: 558 us; the launch traced here: 549 us
  blocking collectives  307 us (55%)
  local copies, waits for them, and re-layouts  114 us (20%)
  matrix products  74.3 us (13%)
  starting transfers between devices  34.3 us (6%)
  other arithmetic  17.7 us (3%)
    all_gather x2, blocking collectives, tree_pass(): lax.all_gather(upper_pair, 'leaf', axis=1, tiled=True)  106 us
    all_gather x2, blocking collectives, tree_pass(): lax.all_gather(subtree_root, 'leaf', axis=1, tiled=True)  91.6 us
    all_gather x2, blocking collectives, tree_pass(): ancestor = lax.all_gather(owned_terms, 'leaf', axis=1, tiled=True)  90.5 us
    unnamed x155, local copies, waits for them, and re-layouts  43 us
    dot_general x12, matrix products, couple_lists(): return jnp.einsum('nkab,cnkb->cna', blocks, picked, precision=highest)  21.4 us
    dot_general x2, matrix products, near_field(): terms = jnp.einsum('pij,rpj->rpi', near_blocks, picked, precision=highest)  19.8 us
    all_gather x2, blocking collectives, apply_matrix(): leaf_coeffs = lax.all_gather(own_coeffs, 'rhs', axis=1, tiled=True)  19.1 us
    gather x12, local copies, waits for them, and re-layouts, couple_lists(): picked = jnp.take(table, clipped, axis=1)  18.1 us
  transfers between devices with their start and end apart: 9, of which 1 were waited for; matrix products, arithmetic and copies ran while one was open for 29% of the time, Pallas kernels for 0%

commit v1 on v0

--- a/solution.py
+++ b/solution.py
@@ -80,7 +80,9 @@
     bordered = with_halo(rims, (("leaf", 2),), 3)
     all_roots, all_pairs = (
         lax.all_gather(subtree_root, "leaf", axis=1, tiled=True),
-        lax.all_gather(upper_pair, "leaf", axis=1, tiled=True),
+        jnp.concatenate(
+            lax.all_to_all(jnp.stack([upper_pair] * lax.axis_size("leaf")), "leaf", 0, 0), axis=1
+        ),
     )
     climbing = {top_depth: all_roots}
     for tree_level in range(top_depth, 0, -1):

time: 558 us -> 480 us (0.86)
  blocking collectives: 307 us -> 206 us
  starting transfers between devices: 34.3 us -> 48.3 us
    all_gather x2 -> x0, blocking collectives: 106 us -> none  [tree_pass(): lax.all_gather(upper_pair, 'leaf', axis=1, tiled=True)]
    all_to_all x0 -> x2, starting transfers between devices: none -> 14.5 us  [tree_pass(): lax.all_to_all(jnp.stack([upper_pair] * lax.axis_size('leaf')), 'leaf', 0...]
    unnamed x155 -> x165, local copies, waits for them, and re-layouts: 43 us -> 48.7 us
  transfers between devices with their start and end apart: 9 -> 11, of which waited for: 1 -> 0; matrix products, arithmetic and copies ran while one was open for 29% -> 37% of each run, Pallas kernels for 0% -> 0%
where the time goes in v1:
time: 480 us; the launch traced here: 470 us
  blocking collectives  206 us (43%)
  local copies, waits for them, and re-layouts  119 us (25%)
  matrix products  73.3 us (15%)
  starting transfers between devices  48.3 us (10%)
  other arithmetic  21.9 us (5%)
    all_gather x2, blocking collectives, tree_pass(): lax.all_gather(subtree_root, 'leaf', axis=1, tiled=True)  97.1 us
    all_gather x2, blocking collectives, tree_pass(): ancestor = lax.all_gather(owned_terms, 'leaf', axis=1, tiled=True)  90.6 us
    unnamed x165, local copies, waits for them, and re-layouts  48.7 us
    dot_general x12, matrix products, couple_lists(): return jnp.einsum('nkab,cnkb->cna', blocks, picked, precision=highest)  20.6 us
    dot_general x2, matrix products, near_field(): terms = jnp.einsum('pij,rpj->rpi', near_blocks, picked, precision=highest)  20.5 us
    all_gather x2, blocking collectives, apply_matrix(): leaf_coeffs = lax.all_gather(own_coeffs, 'rhs', axis=1, tiled=True)  18.5 us
    gather x12, local copies, waits for them, and re-layouts, couple_lists(): picked = jnp.take(table, clipped, axis=1)  18.1 us
    ppermute x4, starting transfers between devices, with_halo(): after = lax.ppermute(leading, axis, down)  17.2 us
  transfers between devices with their start and end apart: 11, of which 0 were waited for; matrix products, arithmetic and copies ran while one was open for 37% of the time, Pallas kernels for 0%

profile of v1, /device:TPU:1, one launch (start us, length us, event | category | flops | bytes accessed | tf_op | source)
XLA Modules:
  0.0 470.5 jit_solution(8486787094770459709)
XLA Ops:
  0.6 1.4 copy.126
  2.1 5.0 %all-to-all-start = ((f32[2,16,256]{2,0,1:T(2,128)}), f32[2,16,256]{2,0,1:T(2,128)}, u32[]{:S(2)}, u32[]{:S(2)}) async-start(f32[2,16,256]{2,0,1:T(2,128)} %copy.126), calls=%async_computation | async-start | bytes 65536 | tf_op jit(solution)/shard_map/all_to_all | solution.py:184
  14.0 13.1 %constant_dynamic-slice_fusion.5 = (f32[1,64,64]{0,2,1:T(8,128)}, f32[1,64,64]{0,2,1:T(8,128)}, f32[1,64,64]{0,2,1:T(8,128)}, f32[1,64,64]{0,2,1:T(8,128)}, f32[1,64,64]{0,2,1:T(8,128)}, /*index=5*/f32[1,64,64]{0,2,1:T(8,128)}) fusion(f32[126,64,64]{0,2,1:T(8,128)} %param.35, s32[]{:T(128)S(6)} %select_n.163, s32[]{:T(128)S(6)} %select_n.162, ...), kind=kLoop, calls=%fused_computation.260 | loop fusion | bytes 196632 | tf_op jit(solution)/shard_map/jit(dynamic_index_in_dim)/dynamic_slice | solution.py:111
  27.2 2.4 copy.183
  35.7 2.0 slice.203
  37.7 1.9 slice.204
  39.6 1.9 slice.205
  41.5 1.9 slice.206
  43.5 1.9 slice.207
  45.4 3.9 copy.177
  49.3 3.4 copy.178
  52.7 3.0 copy.179
  55.7 2.2 copy.180
  58.0 2.9 copy.181
  62.2 3.0 copy.184
  66.5 3.0 copy.186
  69.5 3.0 copy.187
  81.7 9.6 %all_gather.18 = f32[8,16,64]{2,0,1:T(8,128)S(1)} all-gather(f32[8,4,64]{2,0,1:T(8,128)S(1)} %convolution_bitcast_fusion.7), channel_id=1, replica_groups=mesh['leaf'=64,'rhs'=4] {'rhs'}, dimensions={1}, use_global_device_ids=true | all-gather | bytes 40960 | tf_op jit(solution)/shard_map/all_gather | solution.py:151
  94.1 3.1 collective-permute-start
  97.2 7.9 %collective-permute-start.1 = (f32[8,4,256]{2,0,1:T(8,128)}, f32[8,4,256]{2,0,1:T(8,128)}, u32[]{:S(2)}, u32[]{:S(2)}) collective-permute-start(f32[8,4,256]{2,0,1:T(8,128)} %all_to_all.22), channel_id=1, source_target_pairs={{1,0},{2,1},{3,2},{4,3},{5,4},{6,5},{7,6},{8,7},{9,8},{10,9},{11,1... | collective-permute-start | bytes 98312 | tf_op jit(solution)/shard_map/ppermute | solution.py:18
  107.1 47.9 %all-gather.4 = f32[64,64,8]{1,2,0:T(8,128)S(1)} all-gather(f32[1,64,8]{1,2,0:T(8,128)S(1)} %convolution_bitcast_fusion.19), channel_id=2, replica_groups=mesh['leaf'=64,'rhs'=4] {'leaf'}, dimensions={0}, use_global_device_ids=true | all-gather | bytes 133120 | tf_op jit(solution)/shard_map/all_gather | solution.py:82
  155.7 1.7 reshape.363
  157.4 1.7 reshape.336
  159.1 1.9 copy.139
  161.0 2.9 bitcast_reduce_fusion.1
  167.0 2.2 gather_fusion.6
  170.4 43.1 %all-gather.5 = f32[64,64,8]{1,2,0:T(8,128)S(1)} all-gather(f32[1,64,8]{1,2,0:T(8,128)S(1)} %convolution_bitcast_fusion.16), channel_id=3, replica_groups=mesh['leaf'=64,'rhs'=4] {'leaf'}, dimensions={0}, use_global_device_ids=true | all-gather | bytes 133120 | tf_op jit(solution)/shard_map/all_gather | solution.py:103
  214.3 1.7 reshape.365
  216.0 1.7 reshape.337
  217.7 2.1 reshape.441
  219.8 7.4 %all-to-all-start.1 = ((f32[64,1,1024]{2,1,0:T(1,128)}), f32[64,1,1024]{2,1,0:T(1,128)}, u32[]{:S(2)}, u32[]{:S(2)}) async-start(f32[64,1,1024]{2,1,0:T(1,128)} %reshape.441), calls=%async_computation.1 | async-start | bytes 524288 | tf_op jit(solution)/shard_map/all_to_all | solution.py:84
  229.3 3.5 collective-permute-start.2
  232.9 2.3 collective-permute-start.3
  235.2 2.2 gather_fusion.5
  243.2 1.6 fusion.18
  248.1 2.1 gather_fusion.3
  251.6 2.2 gather_fusion.2
  253.8 1.5 pad_maximum_fusion.2
  255.3 2.3 gather_fusion.1
  257.6 3.0 convolution_bitcast_fusion.4
  260.5 4.2 fusion.4
  264.7 1.6 convolution_bitcast_fusion.9
  266.4 1.4 pad_maximum_fusion.1
  267.8 2.3 gather_fusion
  270.1 11.1 %convolution_bitcast_fusion.1 = f32[8,32,256]{2,0,1:T(8,128)} fusion(f32[32,256,256]{2,1,0:T(8,128)} %param.26, f32[32,8,256]{2,1,0:T(8,128)} %gather_fusion, pred[32]{0:T(512)(128)(4,1)} %get-tuple-element.18), kind=kOutput, calls=%fused_computation.19 | convolution fusion | flops 201392128 | bytes 8912928 | tf_op jit(solution)/shard_map/pij,rpj->rpi/dot_general | solution.py:40
  281.8 2.9 reduce.12
  284.6 1.9 reshape.442
  286.5 2.3 gather_fusion.4
  297.0 9.0 %all_gather.21 = f32[8,16,64]{2,0,1:T(8,128)S(1)} all-gather(f32[8,4,64]{2,0,1:T(8,128)S(1)} %convolution_bitcast_fusion.6), channel_id=1, replica_groups=mesh['leaf'=64,'rhs'=4] {'rhs'}, dimensions={1}, use_global_device_ids=true | all-gather | bytes 40960 | tf_op jit(solution)/shard_map/all_gather | solution.py:151
  309.7 49.3 %all-gather.6 = f32[64,64,8]{1,2,0:T(8,128)S(1)} all-gather(f32[1,64,8]{1,2,0:T(8,128)S(1)} %convolution_bitcast_fusion.15), channel_id=4, replica_groups=mesh['leaf'=64,'rhs'=4] {'leaf'}, dimensions={0}, use_global_device_ids=true | all-gather | bytes 133120 | tf_op jit(solution)/shard_map/all_gather | solution.py:82
  359.7 1.7 reshape.367
  361.4 1.7 reshape.338
  363.2 2.9 bitcast_reduce_fusion
  366.4 1.9 collective-permute-start.4
  368.3 4.9 %collective-permute-start.5 = (f32[8,4,256]{2,1,0:T(4,128)}, f32[8,4,256]{2,1,0:T(4,128)S(1)}, u32[]{:S(2)}, u32[]{:S(2)}) collective-permute-start(f32[8,4,256]{2,1,0:T(4,128)} %fusion.13), channel_id=1, source_target_pairs={{1,0},{2,1},{3,2},{4,3},{5,4},{6,5},{7,6},{8,7},{9,8},{10,9},{11,1... | collective-permute-start | bytes 98312 | tf_op jit(solution)/shard_map/ppermute | solution.py:18
  373.3 3.1 collective-permute-start.6
  376.5 2.1 collective-permute-start.7
  384.5 1.6 gather_fusion.13
  386.4 47.5 %all-gather.7 = f32[64,64,8]{1,2,0:T(8,128)S(1)} all-gather(f32[1,64,8]{1,2,0:T(8,128)S(1)} %convolution_bitcast_fusion.12), channel_id=5, replica_groups=mesh['leaf'=64,'rhs'=4] {'leaf'}, dimensions={0}, use_global_device_ids=true | all-gather | bytes 133120 | tf_op jit(solution)/shard_map/all_gather | solution.py:103
  436.2 7.1 %all-to-all-start.2 = ((f32[64,1,1024]{2,1,0:T(1,128)}), f32[64,1,1024]{2,1,0:T(1,128)S(1)}, u32[]{:S(2)}, u32[]{:S(2)}) async-start(f32[64,1,1024]{2,1,0:T(1,128)} %reshape.443), calls=%async_computation.2 | async-start | bytes 524288 | tf_op jit(solution)/shard_map/all_to_all | solution.py:84
  445.0 3.5 fusion.7
  449.7 2.2 convolution_bitcast_fusion.2
  452.0 1.6 convolution_bitcast_fusion.8
  455.2 9.3 %convolution_bitcast_fusion = f32[8,32,256]{2,0,1:T(8,128)S(1)} fusion(f32[32,256,256]{2,1,0:T(8,128)} %param.26, f32[32,8,256]{2,1,0:T(8,128)S(1)} %gather_fusion.7, pred[32]{0:T(512)(128)(4,1)S(1)} %copy-done.56), kind=kOutput, calls=%fused_computation.18 | convolution fusion | flops 201392128 | bytes 8912928 | tf_op jit(solution)/shard_map/pij,rpj->rpi/dot_general | solution.py:40
  (288 shorter events, 79.7 us)
Async XLA Ops:
  0.6 79.8 %copy-start = (f32[4,64,256]{2,1,0:T(8,128)S(1)}, f32[4,64,256]{2,1,0:T(8,128)}, u32[]{:S(2)}) copy-start(f32[4,64,256]{2,1,0:T(8,128)} %param.28) | copy-start | bytes 786436
  2.1 76.9 %all-to-all-start = ((f32[2,16,256]{2,0,1:T(2,128)}), f32[2,16,256]{2,0,1:T(2,128)}, u32[]{:S(2)}, u32[]{:S(2)}) async-start(f32[2,16,256]{2,0,1:T(2,128)} %copy.126), calls=%async_computation | async-start | bytes 65536 | tf_op jit(solution)/shard_map/all_to_all | solution.py:184
  27.2 6.2 %copy-start.65 = (s32[1,4]{1,0:T(1,128)S(1)}, s32[1,4]{1,0:T(1,128)}, u32[]{:S(2)}) copy-start(s32[1,4]{1,0:T(1,128)} %param.37) | copy-start | bytes 52
  27.2 8.6 %copy-start.1 = (f32[126,64,64]{0,2,1:T(8,128)S(1)}, f32[126,64,64]{0,2,1:T(8,128)}, u32[]{:S(2)}) copy-start(f32[126,64,64]{0,2,1:T(8,128)} %param.35) | copy-start | bytes 6193156
  66.5 6.0 %copy-start.6 = (f32[1,64,64]{0,2,1:T(8,128)S(1)}, f32[1,64,64]{0,2,1:T(8,128)}, u32[]{:S(2)}) copy-start(f32[1,64,64]{0,2,1:T(8,128)} %get-tuple-element.20) | copy-start | bytes 49156
  69.5 21.7 %copy-start.3 = (f32[28,64,64]{2,1,0:T(8,128)S(1)}, f32[28,64,64]{2,1,0:T(8,128)}, u32[]{:S(2)}) copy-start(f32[28,64,64]{2,1,0:T(8,128)} %param.29) | copy-start | bytes 1376260
  80.4 80.6 %copy-start.2 = (f32[64,64,64]{2,1,0:T(8,128)S(1)}, f32[64,64,64]{2,1,0:T(8,128)}, u32[]{:S(2)}) copy-start(f32[64,64,64]{2,1,0:T(8,128)} %copy.177) | copy-start | bytes 3145732
  91.2 14.8 %copy-start.19 = (f32[8,16,64]{2,0,1:T(8,128)}, f32[8,16,64]{2,0,1:T(8,128)S(1)}, u32[]{:S(2)}) copy-start(f32[8,16,64]{2,0,1:T(8,128)S(1)} %all_gather.18) | copy-start | bytes 98308
  91.7 14.3 %copy-start.25 = (f32[8,8,64]{2,0,1:T(8,128)}, f32[8,8,64]{2,0,1:T(8,128)S(1)}, u32[]{:S(2)}) copy-start(f32[8,8,64]{2,0,1:T(8,128)S(1)} %bitcast_reduce_fusion.7) | copy-start | bytes 49156
  94.1 172.2 %collective-permute-start = (f32[8,4,256]{2,0,1:T(8,128)}, f32[8,4,256]{2,0,1:T(8,128)}, u32[]{:S(2)}, u32[]{:S(2)}) collective-permute-start(f32[8,4,256]{2,0,1:T(8,128)} %all_to_all.22), channel_id=1, source_target_pairs={{0,1},{1,2},{2,3},{3,4},{4,5},{5,6},{6,7},{7,8},{8,9},{9,10},{10,1... | collective-permute-start | bytes 98312 | tf_op jit(solution)/shard_map/ppermute | solution.py:17
  97.2 169.1 %collective-permute-start.1 = (f32[8,4,256]{2,0,1:T(8,128)}, f32[8,4,256]{2,0,1:T(8,128)}, u32[]{:S(2)}, u32[]{:S(2)}) collective-permute-start(f32[8,4,256]{2,0,1:T(8,128)} %all_to_all.22), channel_id=1, source_target_pairs={{1,0},{2,1},{3,2},{4,3},{5,4},{6,5},{7,6},{8,7},{9,8},{10,9},{11,1... | collective-permute-start | bytes 98312 | tf_op jit(solution)/shard_map/ppermute | solution.py:18
  159.1 5.8 %copy-start.8 = (f32[16,64,64]{2,1,0:T(8,128)S(1)}, f32[16,64,64]{2,1,0:T(8,128)}, u32[]{:S(2)}) copy-start(f32[16,64,64]{2,1,0:T(8,128)} %copy.179) | copy-start | bytes 786436
  219.8 61.5 %all-to-all-start.1 = ((f32[64,1,1024]{2,1,0:T(1,128)}), f32[64,1,1024]{2,1,0:T(1,128)}, u32[]{:S(2)}, u32[]{:S(2)}) async-start(f32[64,1,1024]{2,1,0:T(1,128)} %reshape.441), calls=%async_computation.1 | async-start | bytes 524288 | tf_op jit(solution)/shard_map/all_to_all | solution.py:84
  229.3 15.4 %collective-permute-start.2 = (f32[8,3,3,64]{3,0,2,1:T(8,128)}, f32[8,3,3,64]{3,0,2,1:T(8,128)}, u32[]{:S(2)}, u32[]{:S(2)}) collective-permute-start(f32[8,3,3,64]{3,0,2,1:T(8,128)} %get-tuple-element.38), channel_id=1, source_target_pairs={{0,4},{4,8},{8,12},{12,16},{16,20},{20,24},{24,28},{28,32},{32,36}... | collective-permute-start | bytes 55304 | tf_op jit(solution)/shard_map/ppermute | solution.py:17
  232.9 13.3 %collective-permute-start.3 = (f32[8,3,3,64]{3,0,2,1:T(8,128)}, f32[8,3,3,64]{3,0,2,1:T(8,128)}, u32[]{:S(2)}, u32[]{:S(2)}) collective-permute-start(f32[8,3,3,64]{3,0,2,1:T(8,128)} %get-tuple-element.39), channel_id=1, source_target_pairs={{4,0},{8,4},{12,8},{16,12},{20,16},{24,20},{28,24},{32,28},{36,32}... | collective-permute-start | bytes 55304 | tf_op jit(solution)/shard_map/ppermute | solution.py:18
  248.1 12.4 %copy-start.34 = (f32[16,4]{1,0:T(8,128)S(1)}, f32[16,4]{1,0:T(8,128)}, u32[]{:S(2)}) copy-start(f32[16,4]{1,0:T(8,128)} %copy.131) | copy-start | bytes 772
  248.1 12.4 %copy-start.49 = (pred[16,4]{1,0:T(8,128)(4,1)S(1)}, pred[16,4]{1,0:T(8,128)(4,1)}, u32[]{:S(2)}) copy-start(pred[16,4]{1,0:T(8,128)(4,1)} %copy.129) | copy-start | bytes 196
  257.6 7.2 %copy-start.32 = (f32[16,8,64]{2,1,0:T(8,128)S(1)}, f32[16,8,64]{2,1,0:T(8,128)}, u32[]{:S(2)}) copy-start(f32[16,8,64]{2,1,0:T(8,128)} %gather_fusion.3) | copy-start | bytes 98308
  257.6 8.8 %copy-start.31 = (f32[8,4,256]{2,0,1:T(8,128)S(1)}, f32[8,4,256]{2,0,1:T(8,128)}, u32[]{:S(2)}) copy-start(f32[8,4,256]{2,0,1:T(8,128)} %all_to_all.22) | copy-start | bytes 98308
  288.8 6.1 %copy-start.14 = (f32[8,32,256]{2,0,1:T(8,128)S(1)}, f32[8,32,256]{2,0,1:T(8,128)}, u32[]{:S(2)}) copy-start(f32[8,32,256]{2,0,1:T(8,128)} %convolution_bitcast_fusion.1) | copy-start | bytes 786436
  288.8 6.1 %copy-start.58 = (s32[32]{0:T(128)S(1)}, s32[32]{0:T(128)}, u32[]{:S(2)}) copy-start(s32[32]{0:T(128)} %subtract_bitcast_fusion) | copy-start | bytes 388
  288.8 20.7 %copy-start.15 = (f32[2,64,64]{2,1,0:T(8,128)S(1)}, f32[2,64,64]{2,1,0:T(8,128)}, u32[]{:S(2)}) copy-start(f32[2,64,64]{2,1,0:T(8,128)} %param.32) | copy-start | bytes 98308
  363.1 10.1 %copy-start.42 = (f32[8,3,64]{2,0,1:T(8,128)S(1)}, f32[8,3,64]{2,0,1:T(8,128)}, u32[]{:S(2)}) copy-start(f32[8,3,64]{2,0,1:T(8,128)} %get-tuple-element.60) | copy-start | bytes 18436
  363.1 10.1 %copy-start.43 = (f32[8,3,64]{2,0,1:T(8,128)S(1)}, f32[8,3,64]{2,0,1:T(8,128)}, u32[]{:S(2)}) copy-start(f32[8,3,64]{2,0,1:T(8,128)} %get-tuple-element.61) | copy-start | bytes 18436
  363.1 10.1 %copy-start.40 = (f32[8,3,64]{2,0,1:T(8,128)S(1)}, f32[8,3,64]{2,0,1:T(8,128)}, u32[]{:S(2)}) copy-start(f32[8,3,64]{2,0,1:T(8,128)} %get-tuple-element.56) | copy-start | bytes 18436
  363.1 10.1 %copy-start.41 = (f32[8,3,64]{2,0,1:T(8,128)S(1)}, f32[8,3,64]{2,0,1:T(8,128)}, u32[]{:S(2)}) copy-start(f32[8,3,64]{2,0,1:T(8,128)} %get-tuple-element.57) | copy-start | bytes 18436
  363.2 10.1 %copy-start.38 = (f32[8,3,64]{2,0,1:T(8,128)S(1)}, f32[8,3,64]{2,0,1:T(8,128)}, u32[]{:S(2)}) copy-start(f32[8,3,64]{2,0,1:T(8,128)} %get-tuple-element.40) | copy-start | bytes 18436
  363.2 10.1 %copy-start.39 = (f32[8,3,64]{2,0,1:T(8,128)S(1)}, f32[8,3,64]{2,0,1:T(8,128)}, u32[]{:S(2)}) copy-start(f32[8,3,64]{2,0,1:T(8,128)} %get-tuple-element.41) | copy-start | bytes 18436
  363.2 15.3 %copy-start.5 = (f32[32,64,64]{2,1,0:T(8,128)S(1)}, f32[32,64,64]{2,1,0:T(8,128)}, u32[]{:S(2)}) copy-start(f32[32,64,64]{2,1,0:T(8,128)} %copy.178) | copy-start | bytes 1572868
  363.2 16.3 %copy-start.9 = (f32[16,64,64]{2,1,0:T(8,128)S(1)}, f32[16,64,64]{2,1,0:T(8,128)}, u32[]{:S(2)}) copy-start(f32[16,64,64]{2,1,0:T(8,128)} %copy.179) | copy-start | bytes 786436
  366.1 14.2 %copy-start.13 = (f32[4,64,64]{2,1,0:T(8,128)S(1)}, f32[4,64,64]{2,1,0:T(8,128)}, u32[]{:S(2)}) copy-start(f32[4,64,64]{2,1,0:T(8,128)} %copy.181) | copy-start | bytes 196612
  366.2 14.5 %copy-start.21 = (f32[2,64,64]{2,1,0:T(8,128)S(1)}, f32[2,64,64]{2,1,0:T(8,128)}, u32[]{:S(2)}) copy-start(f32[2,64,64]{2,1,0:T(8,128)} %copy.182) | copy-start | bytes 98308
  366.3 19.8 %copy-start.22 = (f32[1,4,64,64]{3,2,1,0:T(8,128)S(1)}, f32[1,4,64,64]{3,2,1,0:T(8,128)}, u32[]{:S(2)}) copy-start(f32[1,4,64,64]{3,2,1,0:T(8,128)} %param.36) | copy-start | bytes 196612
  366.4 19.8 %copy-start.54 = (pred[4]{0:T(512)(128)(4,1)S(1)}, pred[4]{0:T(512)(128)(4,1)}, u32[]{:S(2)}) copy-start(pred[4]{0:T(512)(128)(4,1)} %get-tuple-element.8) | copy-start | bytes 16
  366.4 19.8 %copy-start.55 = (f32[4]{0:T(128)S(1)}, f32[4]{0:T(128)}, u32[]{:S(2)}) copy-start(f32[4]{0:T(128)} %get-tuple-element.70) | copy-start | bytes 52
  366.4 87.2 %collective-permute-start.4 = (f32[8,4,256]{2,1,0:T(4,128)}, f32[8,4,256]{2,1,0:T(4,128)S(1)}, u32[]{:S(2)}, u32[]{:S(2)}) collective-permute-start(f32[8,4,256]{2,1,0:T(4,128)} %fusion.13), channel_id=1, source_target_pairs={{0,1},{1,2},{2,3},{3,4},{4,5},{5,6},{6,7},{7,8},{8,9},{9,10},{10,1... | collective-permute-start | bytes 98312 | tf_op jit(solution)/shard_map/ppermute | solution.py:17
  368.3 85.3 %collective-permute-start.5 = (f32[8,4,256]{2,1,0:T(4,128)}, f32[8,4,256]{2,1,0:T(4,128)S(1)}, u32[]{:S(2)}, u32[]{:S(2)}) collective-permute-start(f32[8,4,256]{2,1,0:T(4,128)} %fusion.13), channel_id=1, source_target_pairs={{1,0},{2,1},{3,2},{4,3},{5,4},{6,5},{7,6},{8,7},{9,8},{10,9},{11,1... | collective-permute-start | bytes 98312 | tf_op jit(solution)/shard_map/ppermute | solution.py:18
  373.3 70.9 %collective-permute-start.6 = (f32[8,3,3,64]{3,0,2,1:T(8,128)S(1)}, f32[8,3,3,64]{3,0,2,1:T(8,128)S(1)}, u32[]{:S(2)}, u32[]{:S(2)}) collective-permute-start(f32[8,3,3,64]{3,0,2,1:T(8,128)S(1)} %get-tuple-element.36), channel_id=1, source_target_pairs={{0,4},{4,8},{8,12},{12,16},{16,20},{20,24},{24,28},{28,32},{32,36}... | collective-permute-start | bytes 55304 | tf_op jit(solution)/shard_map/ppermute | solution.py:17
  376.4 58.5 %copy-start.11 = (f32[3,4,64,64]{3,2,1,0:T(8,128)S(1)}, f32[3,4,64,64]{3,2,1,0:T(8,128)}, u32[]{:S(2)}) copy-start(f32[3,4,64,64]{3,2,1,0:T(8,128)} %param.33) | copy-start | bytes 589828
  376.4 58.5 %copy-start.60 = (pred[4]{0:T(512)(128)(4,1)S(1)}, pred[4]{0:T(512)(128)(4,1)}, u32[]{:S(2)}) copy-start(pred[4]{0:T(512)(128)(4,1)} %get-tuple-element.65) | copy-start | bytes 16
  376.4 58.5 %copy-start.61 = (f32[4]{0:T(128)S(1)}, f32[4]{0:T(128)}, u32[]{:S(2)}) copy-start(f32[4]{0:T(128)} %get-tuple-element.66) | copy-start | bytes 52
  376.5 67.8 %collective-permute-start.7 = (f32[8,3,3,64]{3,0,2,1:T(8,128)S(1)}, f32[8,3,3,64]{3,0,2,1:T(8,128)S(1)}, u32[]{:S(2)}, u32[]{:S(2)}) collective-permute-start(f32[8,3,3,64]{3,0,2,1:T(8,128)S(1)} %get-tuple-element.37), channel_id=1, source_target_pairs={{4,0},{8,4},{12,8},{16,12},{20,16},{24,20},{28,24},{32,28},{36,32}... | collective-permute-start | bytes 55304 | tf_op jit(solution)/shard_map/ppermute | solution.py:18
  380.4 63.0 %copy-start.30 = (f32[1,64,64]{2,1,0:T(8,128)S(1)}, f32[1,64,64]{2,1,0:T(8,128)}, u32[]{:S(2)}) copy-start(f32[1,64,64]{2,1,0:T(8,128)} %copy.184) | copy-start | bytes 49156
  380.4 63.0 %copy-start.46 = (f32[8,64]{1,0:T(8,128)S(1)}, f32[8,64]{1,0:T(8,128)}, u32[]{:S(2)}) copy-start(f32[8,64]{1,0:T(8,128)} %fusion.90) | copy-start | bytes 6148
  380.4 63.2 %copy-start.29 = (f32[1,64,64]{2,1,0:T(8,128)S(1)}, f32[1,64,64]{2,1,0:T(8,128)}, u32[]{:S(2)}) copy-start(f32[1,64,64]{2,1,0:T(8,128)} %copy.185) | copy-start | bytes 49156
  380.4 63.3 %copy-start.28 = (f32[1,64,64]{2,1,0:T(8,128)S(1)}, f32[1,64,64]{2,1,0:T(8,128)}, u32[]{:S(2)}) copy-start(f32[1,64,64]{2,1,0:T(8,128)} %copy.186) | copy-start | bytes 49156
  380.4 63.5 %copy-start.27 = (f32[1,64,64]{2,1,0:T(8,128)S(1)}, f32[1,64,64]{2,1,0:T(8,128)}, u32[]{:S(2)}) copy-start(f32[1,64,64]{2,1,0:T(8,128)} %copy.187) | copy-start | bytes 49156
  380.4 63.7 %copy-start.26 = (f32[1,64,64]{2,1,0:T(8,128)S(1)}, f32[1,64,64]{2,1,0:T(8,128)}, u32[]{:S(2)}) copy-start(f32[1,64,64]{2,1,0:T(8,128)} %copy.188) | copy-start | bytes 49156
  382.0 62.3 %copy-start.18 = (f32[8,16,64]{2,0,1:T(8,128)S(1)}, f32[8,16,64]{2,0,1:T(8,128)}, u32[]{:S(2)}) copy-start(f32[8,16,64]{2,0,1:T(8,128)} %copy-done.17) | copy-start | bytes 98308
  383.9 60.5 %copy-start.33 = (s32[1024]{0:T(1024)S(1)}, s32[1024]{0:T(1024)}, u32[]{:S(2)}) copy-start(s32[1024]{0:T(1024)} %get-tuple-element.74) | copy-start | bytes 12292
  386.4 58.6 %copy-start.35 = (f32[16,4]{1,0:T(8,128)S(1)}, f32[16,4]{1,0:T(8,128)}, u32[]{:S(2)}) copy-start(f32[16,4]{1,0:T(8,128)} %copy.131) | copy-start | bytes 772
  386.4 58.6 %copy-start.50 = (pred[16,4]{1,0:T(8,128)(4,1)S(1)}, pred[16,4]{1,0:T(8,128)(4,1)}, u32[]{:S(2)}) copy-start(pred[16,4]{1,0:T(8,128)(4,1)} %copy.129) | copy-start | bytes 196
  436.2 12.3 %copy-start.51 = (s32[1024]{0:T(1024)S(1)}, s32[1024]{0:T(1024)}, u32[]{:S(2)}) copy-start(s32[1024]{0:T(1024)} %pad_clamp_fusion.3) | copy-start | bytes 12292
  436.2 12.9 %copy-start.24 = (f32[8,8,64]{2,0,1:T(8,128)S(1)}, f32[8,8,64]{2,0,1:T(8,128)}, u32[]{:S(2)}) copy-start(f32[8,8,64]{2,0,1:T(8,128)} %copy-done.23) | copy-start | bytes 49156
  436.2 12.9 %copy-start.44 = (s32[1024]{0:T(1024)S(1)}, s32[1024]{0:T(1024)}, u32[]{:S(2)}) copy-start(s32[1024]{0:T(1024)} %get-tuple-element.73) | copy-start | bytes 12292
  436.2 28.4 %all-to-all-start.2 = ((f32[64,1,1024]{2,1,0:T(1,128)}), f32[64,1,1024]{2,1,0:T(1,128)S(1)}, u32[]{:S(2)}, u32[]{:S(2)}) async-start(f32[64,1,1024]{2,1,0:T(1,128)} %reshape.443), calls=%async_computation.2 | async-start | bytes 524288 | tf_op jit(solution)/shard_map/all_to_all | solution.py:84
  443.4 6.4 %copy-start.45 = (f32[8,4]{1,0:T(8,128)S(1)}, f32[8,4]{1,0:T(8,128)}, u32[]{:S(2)}) copy-start(f32[8,4]{1,0:T(8,128)} %copy.134) | copy-start | bytes 388
  443.4 6.4 %copy-start.57 = (pred[8,4]{1,0:T(8,128)(4,1)S(1)}, pred[8,4]{1,0:T(8,128)(4,1)}, u32[]{:S(2)}) copy-start(pred[8,4]{1,0:T(8,128)(4,1)} %copy.132) | copy-start | bytes 100
  445.0 7.0 %copy-start.47 = (f32[4,4]{1,0:T(4,128)S(1)}, f32[4,4]{1,0:T(4,128)}, u32[]{:S(2)}) copy-start(f32[4,4]{1,0:T(4,128)} %copy.137) | copy-start | bytes 196
  445.0 7.0 %copy-start.62 = (pred[4,4]{1,0:T(4,128)(4,1)S(1)}, pred[4,4]{1,0:T(4,128)(4,1)}, u32[]{:S(2)}) copy-start(pred[4,4]{1,0:T(4,128)(4,1)} %copy.135) | copy-start | bytes 52
  448.5 6.7 %copy-start.56 = (pred[32]{0:T(512)(128)(4,1)S(1)}, pred[32]{0:T(512)(128)(4,1)}, u32[]{:S(2)}) copy-start(pred[32]{0:T(512)(128)(4,1)} %get-tuple-element.18) | copy-start | bytes 100
  455.2 11.4 %copy-start.52 = (f32[2,4]{1,0:T(2,128)S(1)}, f32[2,4]{1,0:T(2,128)}, u32[]{:S(2)}) copy-start(f32[2,4]{1,0:T(2,128)} %get-tuple-element.67) | copy-start | bytes 100
  455.2 11.4 %copy-start.53 = (pred[2,4]{1,0:T(4,128)(4,1)S(1)}, pred[2,4]{1,0:T(4,128)(4,1)}, u32[]{:S(2)}) copy-start(pred[2,4]{1,0:T(4,128)(4,1)} %get-tuple-element.12) | copy-start | bytes 28
  455.2 11.8 %copy-start.16 = (f32[2,64,64]{2,1,0:T(8,128)S(1)}, f32[2,64,64]{2,1,0:T(8,128)}, u32[]{:S(2)}) copy-start(f32[2,64,64]{2,1,0:T(8,128)} %param.32) | copy-start | bytes 98308
  (13 other events, 43.8 us)
